TPU v7x, 32 devices: a whole 2x2x4 slice. The times are simulated.
32 devices in a mesh: frame: 8 (over z, x), rec: 4 (over y, core).
Axes of the slice: x: 2, y: 2, z: 4, core: 2. Of those that a mesh axis runs over, the one named last changes fastest.
Arguments:
- inputs: bfloat16 [4, 8192, 512], P('rec', 'frame'), may hold values from -6 to 6
- conv_weight: bfloat16 [5, 512, 512], replicated, may hold values from -4 to 4
- conv_bias: float32 [512], replicated, may hold values from -3 to 3
- labels: int32 [4, 8192, 512], P('rec', 'frame'), may hold values 0 or 1
- rec_span: int32 [2, 4, 8192], P(None, 'rec', 'frame'), may hold values from 0 to 1023, as said below
Outputs:
- features: bfloat16 [4, 8192, 512], P('rec', 'frame')
- probe_weights: float32 [512, 512], replicated
Inputs may be any that keep to these rules, and one draw needn't show every extreme that they name: Each stream is a series of whole recordings of at most 1024 frames, the last one possibly cut by the stream's end: rec_span[0, g, t] counts the frames of t's recording before t and rec_span[1, g, t] those after t within the stream; in every stream some recording has exactly 1024 frames.
All inputs are finite; a program needn't handle non-finite values. No bound on the sum of `labels` on one device may be relied on, other than what follows from the above.
Results may differ from a plain program's by a relative error of at most 0.0035.
The roundings to bfloat16 on the way count: a program that leaves them out, or rounds other values in their place, can miss the bound.
Values may be sent and summed in bfloat16 or wider, within the bound.
A program may use at most 64 MiB of HBM per device.

v0:
```python
import math
import jax
import jax.numpy as jnp
from jax import lax
from jax.experimental import pallas as pl
from jax.experimental.pallas import tpu as pltpu
from jax.sharding import PartitionSpec as P

RIDGE = 0.1
TILE = 128
HI = lax.Precision.HIGHEST
GROUP = 4

def mm(a, b):
    return jnp.dot(a, b, precision=HI, preferred_element_type=jnp.float32)

def mtm(a, b):
    return lax.dot_general(a, b, (((0,), (0,)), ((), ())), precision=HI, preferred_element_type=jnp.float32)

def invert_tile(slabs):
    count = len(slabs)
    width = 8 * count
    lane = lax.broadcasted_iota(jnp.int32, (8, width), 1)
    sub = lax.broadcasted_iota(jnp.int32, (8, width), 0)
    def spread(row):
        return jnp.broadcast_to(row, (8, width))
    for j in range(0, width, GROUP):
        home, base = j // 8, j % 8
        cols = [[jnp.broadcast_to(s[:, j + b:j + b + 1], (8, width)) for b in range(GROUP)] for s in slabs]
        piv = [[spread(cols[home][b][base + a:base + a + 1]) for b in range(GROUP)] for a in range(GROUP)]
        in_group = (lane >= j) & (lane < j + GROUP)
        rows = []
        for a in range(GROUP):
            row = spread(slabs[home][base + a:base + a + 1])
            rows.append(jnp.where(in_group, jnp.where(lane == j + a, 1.0, 0.0), row))
        for a in range(GROUP):
            inv = 1.0 / piv[a][a]
            rows[a] = rows[a] * inv
            for b in range(a + 1, GROUP):
                piv[a][b] = piv[a][b] * inv
            for o in range(GROUP):
                if o != a:
                    f = piv[o][a]
                    rows[o] = rows[o] - f * rows[a]
                    for b in range(a + 1, GROUP):
                        piv[o][b] = piv[o][b] - f * piv[a][b]
        fresh = []
        for i, s in enumerate(slabs):
            v = jnp.where(in_group, 0.0, s)
            for b in range(GROUP):
                v = v - cols[i][b] * rows[b]
            if i == home:
                for a in range(GROUP):
                    v = jnp.where(sub == base + a, rows[a], v)
            fresh.append(v)
        slabs = fresh
    return slabs

def factor(a_ref, inv_ref, w_ref, tile):
    size = a_ref.shape[0]
    n = size // tile
    def step(k, carry):
        at = pl.multiple_of(k * tile, tile)
        slabs = [a_ref[pl.ds(at + 8 * i, 8), pl.ds(at, tile)] for i in range(tile // 8)]
        for i, s in enumerate(invert_tile(slabs)):
            inv_ref[pl.ds(at + 8 * i, 8), :] = s
        for c in range(n - 1):
            @pl.when(k == c)
            def _():
                lo, hi = c * tile, (c + 1) * tile
                row = a_ref[lo:hi, hi:]
                w = mm(inv_ref[lo:hi, :], row)
                w_ref[lo:hi, hi:] = w
                for i in range(c + 1, n):
                    s = slice(i * tile, (i + 1) * tile)
                    a_ref[s, i * tile:] -= mtm(a_ref[lo:hi, s], w[:, (i - c - 1) * tile:])
        return carry
    lax.fori_loop(0, n, step, 0)

def substitute(a_ref, inv_ref, w_ref, x_ref, y_ref, tile):
    size = a_ref.shape[0]
    n = size // tile
    for k in range(n):
        lo, hi = k * tile, (k + 1) * tile
        if k:
            x = x_ref[lo:hi, :] - mtm(w_ref[:lo, lo:hi], y_ref[:lo, :])
        else:
            x = x_ref[lo:hi, :]
        y_ref[lo:hi, :] = x
    for k in reversed(range(n)):
        lo, hi = k * tile, (k + 1) * tile
        y = mm(inv_ref[lo:hi, :], y_ref[lo:hi, :])
        if k < n - 1:
            y = y - mm(w_ref[lo:hi, hi:], y_ref[hi:, :])
        y_ref[lo:hi, :] = y


def bits_of(axis, size):
    return [(axis, 1 << i) for i in range(size.bit_length() - 1)]


class Stream:
    def __init__(self, stages, src, out, inbox, sems):
        self.stages, self.src, self.out, self.inbox, self.sems = stages, src, out, inbox, sems
        self.lo, self.length, self.at, self.used = 0, out.shape[0], 0, 0
        self.held, self.copy = (src, 0), None

    def done(self):
        return self.at == 2 * len(self.stages)

    def start(self):
        count = len(self.stages)
        down = self.at < count
        axis, step = self.stages[self.at if down else 2 * count - 1 - self.at]
        me = lax.axis_index(axis)
        self.bit = lax.rem(me // step, 2)
        peer = me + (1 - 2 * self.bit) * step
        if down:
            half = self.length // 2
            ref, base = self.held
            src = ref.at[pl.ds(base + (1 - self.bit) * half, half)]
            dst = self.inbox.at[pl.ds(self.used, half)]
        else:
            src = dst = self.out.at[pl.ds(self.lo, self.length)]
        self.copy = pltpu.make_async_remote_copy(
            src_ref=src, dst_ref=dst,
            send_sem=self.sems.at[0, self.at], recv_sem=self.sems.at[1, self.at],
            device_id={axis: peer}, device_id_type=pl.DeviceIdType.MESH,
        )
        self.copy.start()

    def finish(self):
        self.copy.wait()
        if self.at < len(self.stages):
            half = self.length // 2
            ref, base = self.held
            total = ref[pl.ds(base + self.bit * half, half)] + self.inbox[pl.ds(self.used, half)]
            self.lo, self.length = self.lo + self.bit * half, half
            if self.at < len(self.stages) - 1:
                self.inbox[pl.ds(self.used, half)] = total
                self.held = (self.inbox, self.used)
            else:
                self.out[pl.ds(self.lo, half)] = total
            self.used += half
        else:
            self.lo, self.length = self.lo - self.bit * self.length, 2 * self.length
        self.at += 1


def greet(stages):
    barrier = pltpu.get_barrier_semaphore()
    for axis, step in stages:
        me = lax.axis_index(axis)
        peer = me + (1 - 2 * lax.rem(me // step, 2)) * step
        pl.semaphore_signal(barrier, inc=1, device_id={axis: peer}, device_id_type=pl.DeviceIdType.MESH)
    pl.semaphore_wait(barrier, len(stages))


def orders(frame_size, rec_size):
    frame, rec = bits_of("frame", frame_size), bits_of("rec", rec_size)
    return rec + frame, rec[:1] + frame + rec[1:]


def reduce_kernel(sizes, g_in, x_in, g_out, x_out, g_box, x_box, g_sem, x_sem):
    one, two = orders(*sizes)
    greet(one)
    streams = [Stream(one, g_in, g_out, g_box, g_sem), Stream(two, x_in, x_out, x_box, x_sem)]
    for s in streams:
        s.start()
    while not all(s.done() for s in streams):
        for s in streams:
            if not s.done():
                s.finish()
                if not s.done():
                    s.start()


def reduce_all(g, x):
    sizes = (lax.axis_size("frame"), lax.axis_size("rec"))
    count = len(orders(*sizes)[0])
    vmem = pl.BlockSpec(memory_space=pltpu.VMEM)
    return pl.pallas_call(
        lambda *refs: reduce_kernel(sizes, *refs),
        out_shape=[jax.ShapeDtypeStruct(v.shape, v.dtype) for v in (g, x)],
        in_specs=[vmem, vmem],
        out_specs=[vmem, vmem],
        scratch_shapes=[
            pltpu.VMEM(g.shape, jnp.float32),
            pltpu.VMEM(x.shape, jnp.float32),
            pltpu.SemaphoreType.DMA((2, 2 * count)),
            pltpu.SemaphoreType.DMA((2, 2 * count)),
        ],
        compiler_params=pltpu.CompilerParams(collective_id=0, has_side_effects=True),
    )(g, x)


def pairs(n):
    return [(i, j) for i in range(n) for j in range(i, n)]


def tile_at(ref, slot):
    units = TILE // 8
    return ref[slot * units:(slot + 1) * units].reshape(TILE, TILE)


def column(totals, i):
    return jnp.broadcast_to(totals[i:i + 1], (TILE, TILE)).T


def solve_kernel(frames, g_ref, x_ref, y_ref, a_ref, inv_ref, w_ref, c_ref):
    size, n = a_ref.shape[0], a_ref.shape[0] // TILE
    m = y_ref.shape[1] // TILE
    units = TILE // 8
    rows = -(-(n + m) // 8)
    first = len(pairs(n)) * units
    totals = g_ref[first:first + rows].reshape(8 * rows, TILE)
    cols = [column(totals, i) for i in range(n)]
    eye = lax.broadcasted_iota(jnp.int32, (TILE, TILE), 0) == lax.broadcasted_iota(jnp.int32, (TILE, TILE), 1)
    for slot, (i, j) in enumerate(pairs(n)):
        v = (tile_at(g_ref, slot) - cols[i] * totals[j:j + 1] / frames) / frames
        if i == j:
            v = v + jnp.where(eye, RIDGE, 0.0)
        a_ref[i * TILE:(i + 1) * TILE, j * TILE:(j + 1) * TILE] = v
    factor(a_ref, inv_ref, w_ref, TILE)
    for i in range(n):
        for j in range(m):
            v = tile_at(x_ref, i * m + j) - cols[i] * totals[n + j:n + j + 1] / frames
            c_ref[i * TILE:(i + 1) * TILE, j * TILE:(j + 1) * TILE] = v / math.sqrt(frames)
    substitute(a_ref, inv_ref, w_ref, c_ref, y_ref, TILE)


def solve(g, x, size, wide, frames):
    vmem = pl.BlockSpec(memory_space=pltpu.VMEM)
    return pl.pallas_call(
        lambda *refs: solve_kernel(frames, *refs),
        out_shape=jax.ShapeDtypeStruct((size, wide), jnp.float32),
        in_specs=[vmem, vmem],
        out_specs=vmem,
        scratch_shapes=[
            pltpu.VMEM((size, size), jnp.float32),
            pltpu.VMEM((size, TILE), jnp.float32),
            pltpu.VMEM((size, size), jnp.float32),
            pltpu.VMEM((size, wide), jnp.float32),
        ],
    )(g, x)


def pad_units(v, devices):
    extra = -v.shape[0] % devices
    return jnp.pad(v, ((0, extra), (0, 0), (0, 0)))


def padded_2(shard, sides, width):
    for axis, dim in sides:
        size, length = (lax.axis_size(axis), shard.shape[dim])
        up = [(i, (i + 1) % size) for i in range(size - 1)]
        down = [(j, i) for i, j in up]
        last = lax.slice_in_dim(shard, length - width, length, axis=dim)
        leading = lax.slice_in_dim(shard, 0, width, axis=dim)
        before = lax.ppermute(last, axis, up)
        after = lax.ppermute(leading, axis, down)
        shard = jnp.concatenate([before, shard, after], axis=dim)
    return shard


def per_device(inputs, conv_weight, conv_bias, labels, rec_span):
    tap_count = conv_weight.shape[0]
    half_width = tap_count // 2
    shard_rows = inputs.shape[1]
    feat_width = conv_weight.shape[2]
    padded = padded_2(inputs, (("frame", 1),), half_width)
    before = rec_span[0, 0]
    frames_after = rec_span[1, 0]
    pieces = []
    for tap_index in range(tap_count):
        offset = tap_index - half_width
        shifted = padded[0, tap_index : tap_index + shard_rows]
        if offset < 0:
            keep_mask = before >= -offset
        elif offset > 0:
            keep_mask = frames_after >= offset
        else:
            keep_mask = before >= 0
        pieces.append(jnp.where(keep_mask[:, None], shifted, jnp.zeros_like(shifted)))
    stacked = jnp.concatenate(pieces, axis=1)
    flat_weight = conv_weight.reshape(tap_count * conv_weight.shape[1], feat_width)
    pre_act = jnp.dot(stacked, flat_weight, preferred_element_type=jnp.float32) + conv_bias
    features = jax.nn.gelu(pre_act, approximate=False).astype(jnp.bfloat16)
    joined = jnp.concatenate([features, labels[0].astype(jnp.bfloat16)], axis=1)
    moments = lax.dot_general(
        features, joined, (((0,), (0,)), ((), ())), preferred_element_type=jnp.float32
    )
    totals = jnp.sum(joined, axis=0, dtype=jnp.float32)
    devices = lax.axis_size("frame") * lax.axis_size("rec")
    frames = float(shard_rows * devices)
    wide = labels.shape[2]
    n, m = feat_width // TILE, wide // TILE
    blocks = moments.reshape(n, TILE, n + m, TILE).transpose(0, 2, 1, 3)
    gram = jnp.concatenate([blocks[i, i:n].reshape(-1, 8, TILE) for i in range(n)])
    sums = totals.reshape(n + m, TILE)
    sums = jnp.pad(sums, ((0, -(n + m) % 8), (0, 0))).reshape(-1, 8, TILE)
    g = pad_units(jnp.concatenate([gram, sums]), devices)
    x = pad_units(blocks[:, n:].reshape(-1, 8, TILE), devices)
    g, x = reduce_all(g, x)
    return (features[None], solve(g, x, feat_width, wide, frames))


def solution(mesh):
    in_specs = (P("rec", "frame", None), P(), P(), P("rec", "frame", None), P(None, "rec", "frame"))
    out_specs = (P("rec", "frame", None), P())
    return jax.shard_map(
        per_device, mesh=mesh, in_specs=in_specs, out_specs=out_specs, check_vma=False
    )
```

profile of v0, /device:TPU:0, one launch (start us, length us, event | category | flops | bytes accessed | tf_op | source)
XLA Modules:
  0.0 119.0 jit_solution(6148462805649799390)
XLA Ops:
  0.6 0.0 copy-start
  0.6 0.9 fusion.26
  1.5 4.9 %collective-permute-start = (bf16[1,2,512]{2,1,0:T(2,128)(2,1)S(1)}, bf16[1,2,512]{2,1,0:T(2,128)(2,1)S(1)}, u32[]{:S(2)}, u32[]{:S(2)}) collective-permute-start(bf16[1,2,512]{2,1,0:T(2,128)(2,1)S(1)} %get-tuple-element.14), channel_id=1, source_target_pairs={{0,4},{4,8},{8,12},{12,16},{16,20},{20,24},{24,28},{1,5},{5,9},{9,... | collective-permute-start | bytes 6152 | tf_op jit(solution)/shard_map/ppermute | solution.py:260
  6.4 1.3 %collective-permute-start.1 = (bf16[1,2,512]{2,1,0:T(2,128)(2,1)S(1)}, bf16[1,2,512]{2,1,0:T(2,128)(2,1)S(1)}, u32[]{:S(2)}, u32[]{:S(2)}) collective-permute-start(bf16[1,2,512]{2,1,0:T(2,128)(2,1)S(1)} %get-tuple-element.13), channel_id=1, source_target_pairs={{4,0},{8,4},{12,8},{16,12},{20,16},{24,20},{28,24},{5,1},{9,5},{13... | collective-permute-start | bytes 6152 | tf_op jit(solution)/shard_map/ppermute | solution.py:261
  7.7 2.3 %constant_dynamic-update-slice_fusion.1 = bf16[1,1026,512]{2,1,0:T(8,128)(2,1)} fusion(bf16[1,1024,512]{2,1,0:T(8,128)(2,1)} %param.5), kind=kLoop, calls=%fused_computation.46 | loop fusion | bytes 2097152
  10.0 2.9 %copy.7 = s32[1,1024,512]{1,2,0:T(8,128)} copy(s32[1,1024,512]{2,1,0:T(8,128)} %param.8) | data formatting | bytes 4194304 | tf_op args[3]
  12.9 1.9 %convert_bitcast_fusion = bf16[1024,512]{0,1:T(8,128)(2,1)S(1)} fusion(s32[1,1024,512]{1,2,0:T(8,128)} %copy.7), kind=kLoop, calls=%fused_computation.42 | loop fusion | flops 524288 | bytes 3145728 | tf_op jit(solution)/shard_map/convert_element_type | solution.py:289
  14.8 0.0 copy-done.4
  14.9 0.1 compare_reduce_fusion
  14.9 0.0 collective-permute-done
  14.9 0.0 copy-done.1
  14.9 0.3 fusion.15
  15.3 0.0 copy-start.2
  15.3 0.3 fusion.22
  15.7 0.3 fusion.23
  16.0 0.0 collective-permute-done.1
  16.0 0.5 copy-done.2
  16.5 0.3 fusion.19
  16.9 0.3 fusion.17
  17.2 0.0 copy-done
  17.2 0.0 copy-done.5
  17.3 7.5 %fusion.2 = bf16[1024,512]{0,1:T(8,128)(2,1)S(1)} fusion(bf16[1024,2560]{1,0:T(8,128)(2,1)S(1)} %fusion.17, bf16[2560,512]{1,0:T(8,128)(2,1)S(1)} %bitcast.52, f32[512]{0:T(512)S(1)} %copy-done.5), kind=kOutput, calls=%fused_computation.4 | convolution fusion | flops 2718957568 | bytes 8914944 | tf_op jit(solution)/shard_map/dot_general | solution.py:287
  24.8 0.0 copy-start.3
  24.8 1.3 %fusion.11 = f32[64,8,8,128]{3,1,2,0:T(8,128)S(1)} fusion(bf16[1024,512]{0,1:T(8,128)(2,1)S(1)} %fusion.2, bf16[1024,512]{0,1:T(8,128)(2,1)S(1)} %convert_bitcast_fusion), kind=kOutput, calls=%fused_computation.23 | convolution fusion | flops 1077936128 | bytes 4194304 | tf_op jit(solution)/shard_map/dot_general | solution.py:290
  26.1 0.5 copy.10
  26.6 0.4 copy.12
  27.1 0.3 convert_reduce_fusion
  27.4 1.1 slice.64
  28.6 2.3 %copy.9 = bf16[1,1024,512]{2,1,0:T(8,128)(2,1)} copy(bf16[1,1024,512]{1,2,0:T(8,128)(2,1)} %bitcast.60) | data formatting | bytes 2097152
  30.8 0.9 pad.4.refs_0_
  31.8 47.5 %shard_map.68 = (f32[192,8,128]{2,1,0:T(8,128)}, f32[256,8,128]{2,1,0:T(8,128)}) custom-call(f32[192,8,128]{2,1,0:T(8,128)} %pad.4.refs_0_, f32[256,8,128]{2,1,0:T(8,128)} %bitcast.59), custom_call_target="tpu_custom_call" | custom-call | tf_op jit(solution)/shard_map/pallas_call | solution.py:182
  79.3 39.8 %shard_map.69 = f32[512,512]{1,0:T(8,128)} custom-call(f32[192,8,128]{2,1,0:T(8,128)} %get-tuple-element.4.refs_0_, f32[256,8,128]{2,1,0:T(8,128)} %get-tuple-element.5.refs_1_), custom_call_target="tpu_custom_call" | custom-call | tf_op jit(solution)/shard_map/pallas_call | solution.py:234
  (13 shorter events, 0.1 us)
Async XLA Ops:
  0.6 16.6 %copy-start = (bf16[5,512,512]{2,1,0:T(8,128)(2,1)S(1)}, bf16[5,512,512]{2,1,0:T(8,128)(2,1)}, u32[]{:S(2)}) copy-start(bf16[5,512,512]{2,1,0:T(8,128)(2,1)} %param.6) | copy-start | bytes 7864324
  1.5 13.4 %collective-permute-start = (bf16[1,2,512]{2,1,0:T(2,128)(2,1)S(1)}, bf16[1,2,512]{2,1,0:T(2,128)(2,1)S(1)}, u32[]{:S(2)}, u32[]{:S(2)}) collective-permute-start(bf16[1,2,512]{2,1,0:T(2,128)(2,1)S(1)} %get-tuple-element.14), channel_id=1, source_target_pairs={{0,4},{4,8},{8,12},{12,16},{16,20},{20,24},{24,28},{1,5},{5,9},{9,... | collective-permute-start | bytes 6152 | tf_op jit(solution)/shard_map/ppermute | solution.py:260
  6.4 9.6 %collective-permute-start.1 = (bf16[1,2,512]{2,1,0:T(2,128)(2,1)S(1)}, bf16[1,2,512]{2,1,0:T(2,128)(2,1)S(1)}, u32[]{:S(2)}, u32[]{:S(2)}) collective-permute-start(bf16[1,2,512]{2,1,0:T(2,128)(2,1)S(1)} %get-tuple-element.13), channel_id=1, source_target_pairs={{4,0},{8,4},{12,8},{16,12},{20,16},{24,20},{28,24},{5,1},{9,5},{13... | collective-permute-start | bytes 6152 | tf_op jit(solution)/shard_map/ppermute | solution.py:261
  12.9 1.9 %copy-start.4 = (s32[2,1,1024]{2,1,0:T(1,128)S(1)}, s32[2,1,1024]{2,1,0:T(1,128)}, u32[]{:S(2)}) copy-start(s32[2,1,1024]{2,1,0:T(1,128)} %param.9) | copy-start | bytes 24580
  12.9 2.0 %copy-start.1 = (bf16[1,1024,512]{2,1,0:T(8,128)(2,1)S(1)}, bf16[1,1024,512]{2,1,0:T(8,128)(2,1)}, u32[]{:S(2)}) copy-start(bf16[1,1024,512]{2,1,0:T(8,128)(2,1)} %param.5) | copy-start | bytes 3145732
  15.3 1.2 %copy-start.2 = (bf16[1,1026,512]{2,1,0:T(8,128)(2,1)S(1)}, bf16[1,1026,512]{2,1,0:T(8,128)(2,1)}, u32[]{:S(2)}) copy-start(bf16[1,1026,512]{2,1,0:T(8,128)(2,1)} %constant_dynamic-update-slice_fusion.1) | copy-start | bytes 3151876
  16.5 0.7 copy-start.5
  24.8 2.2 %copy-start.3 = (bf16[1024,512]{0,1:T(8,128)(2,1)}, bf16[1024,512]{0,1:T(8,128)(2,1)S(1)}, u32[]{:S(2)}) copy-start(bf16[1024,512]{0,1:T(8,128)(2,1)S(1)} %fusion.2) | copy-start | bytes 3145732
where the time goes:
time: 119 us
  Pallas kernels  87.3 us (73%)
  local copies, waits for them, and re-layouts  11.9 us (10%)
  matrix products  8.84 us (7%)
  starting transfers between devices  6.15 us (5%)
  other arithmetic  4.02 us (3%)
    pallas_call x1, Pallas kernels, reduce_all(): pl.pallas_call(lambda *refs: reduce_kernel(sizes, *refs), out_shape=[jax....  47.5 us
    pallas_call x1, Pallas kernels, solve(): pl.pallas_call(lambda *refs: solve_kernel(frames, *refs), out_shape=jax.S...  39.8 us
    unnamed x20, local copies, waits for them, and re-layouts  8.59 us
    dot_general x1, matrix products, per_device(): jnp.dot(stacked, flat_weight, preferred_element_type=jnp.float32)  7.55 us
    ppermute x1, starting transfers between devices, padded_2(): before = lax.ppermute(last, axis, up)  4.86 us
  transfers between devices with their start and end apart: 2, of which 0 were waited for; matrix products, arithmetic and copies ran while one was open for 7% of the time, Pallas kernels for 0%

commit v1 on v0

--- a/solution.py
+++ b/solution.py
@@ -8,6 +8,7 @@
 
 RIDGE = 0.1
 TILE = 128
+POINTS = 4
 HI = lax.Precision.HIGHEST
 GROUP = 4
 
@@ -17,7 +18,7 @@
 def mtm(a, b):
     return lax.dot_general(a, b, (((0,), (0,)), ((), ())), precision=HI, preferred_element_type=jnp.float32)
 
-def invert_tile(slabs):
+def invert_tile(slabs, hook):
     count = len(slabs)
     width = 8 * count
     lane = lax.broadcasted_iota(jnp.int32, (8, width), 1)
@@ -54,15 +55,17 @@
                     v = jnp.where(sub == base + a, rows[a], v)
             fresh.append(v)
         slabs = fresh
+        if (j + GROUP) * POINTS % width == 0:
+            hook((j + GROUP) * POINTS // width - 1)
     return slabs
 
-def factor(a_ref, inv_ref, w_ref, tile):
+def factor(a_ref, inv_ref, w_ref, tile, hook):
     size = a_ref.shape[0]
     n = size // tile
     def step(k, carry):
         at = pl.multiple_of(k * tile, tile)
         slabs = [a_ref[pl.ds(at + 8 * i, 8), pl.ds(at, tile)] for i in range(tile // 8)]
-        for i, s in enumerate(invert_tile(slabs)):
+        for i, s in enumerate(invert_tile(slabs, lambda p: hook(k, p))):
             inv_ref[pl.ds(at + 8 * i, 8), :] = s
         for c in range(n - 1):
             @pl.when(k == c)
@@ -101,50 +104,46 @@
 
 class Stream:
     def __init__(self, stages, src, out, inbox, sems):
-        self.stages, self.src, self.out, self.inbox, self.sems = stages, src, out, inbox, sems
-        self.lo, self.length, self.at, self.used = 0, out.shape[0], 0, 0
-        self.held, self.copy = (src, 0), None
-
-    def done(self):
-        return self.at == 2 * len(self.stages)
-
-    def start(self):
-        count = len(self.stages)
-        down = self.at < count
-        axis, step = self.stages[self.at if down else 2 * count - 1 - self.at]
-        me = lax.axis_index(axis)
-        self.bit = lax.rem(me // step, 2)
-        peer = me + (1 - 2 * self.bit) * step
-        if down:
-            half = self.length // 2
-            ref, base = self.held
-            src = ref.at[pl.ds(base + (1 - self.bit) * half, half)]
-            dst = self.inbox.at[pl.ds(self.used, half)]
-        else:
-            src = dst = self.out.at[pl.ds(self.lo, self.length)]
-        self.copy = pltpu.make_async_remote_copy(
-            src_ref=src, dst_ref=dst,
-            send_sem=self.sems.at[0, self.at], recv_sem=self.sems.at[1, self.at],
-            device_id={axis: peer}, device_id_type=pl.DeviceIdType.MESH,
+        self.sems, self.plan = sems, []
+        ref, base, lo, length, used = src, 0, 0, out.shape[0], 0
+        bits = []
+        for at, (axis, step) in enumerate(stages):
+            me = lax.axis_index(axis)
+            bit = lax.rem(me // step, 2)
+            bits.append(bit)
+            half = length // 2
+            where = {axis: me + (1 - 2 * bit) * step}
+            send = (ref, base + (1 - bit) * half, inbox, used, half, where)
+            lo = lo + bit * half
+            last = at == len(stages) - 1
+            into = (out, lo) if last else (inbox, used)
+            self.plan.append((send, (ref, base + bit * half, inbox, used, half) + into))
+            ref, base, length = inbox, used, half
+            used += half
+        for (axis, step), bit in reversed(list(zip(stages, bits))):
+            me = lax.axis_index(axis)
+            where = {axis: me + (1 - 2 * bit) * step}
+            self.plan.append(((out, lo, out, lo, length, where), None))
+            lo, length = lo - bit * length, 2 * length
+
+    def copy(self, at):
+        src, s, dst, d, size, where = self.plan[at][0]
+        return pltpu.make_async_remote_copy(
+            src_ref=src.at[pl.ds(s, size)], dst_ref=dst.at[pl.ds(d, size)],
+            send_sem=self.sems.at[0, at], recv_sem=self.sems.at[1, at],
+            device_id=where, device_id_type=pl.DeviceIdType.MESH,
         )
-        self.copy.start()
-
-    def finish(self):
-        self.copy.wait()
-        if self.at < len(self.stages):
-            half = self.length // 2
-            ref, base = self.held
-            total = ref[pl.ds(base + self.bit * half, half)] + self.inbox[pl.ds(self.used, half)]
-            self.lo, self.length = self.lo + self.bit * half, half
-            if self.at < len(self.stages) - 1:
-                self.inbox[pl.ds(self.used, half)] = total
-                self.held = (self.inbox, self.used)
-            else:
-                self.out[pl.ds(self.lo, half)] = total
-            self.used += half
-        else:
-            self.lo, self.length = self.lo - self.bit * self.length, 2 * self.length
-        self.at += 1
+
+    def start(self, at):
+        if at < len(self.plan):
+            self.copy(at).start()
+
+    def finish(self, at):
+        self.copy(at).wait()
+        add = self.plan[at][1]
+        if add is not None:
+            ref, r, box, b, size, out, o = add
+            out[pl.ds(o, size)] = ref[pl.ds(r, size)] + box[pl.ds(b, size)]
 
 
 def greet(stages):
@@ -161,39 +160,6 @@
     return rec + frame, rec[:1] + frame + rec[1:]
 
 
-def reduce_kernel(sizes, g_in, x_in, g_out, x_out, g_box, x_box, g_sem, x_sem):
-    one, two = orders(*sizes)
-    greet(one)
-    streams = [Stream(one, g_in, g_out, g_box, g_sem), Stream(two, x_in, x_out, x_box, x_sem)]
-    for s in streams:
-        s.start()
-    while not all(s.done() for s in streams):
-        for s in streams:
-            if not s.done():
-                s.finish()
-                if not s.done():
-                    s.start()
-
-
-def reduce_all(g, x):
-    sizes = (lax.axis_size("frame"), lax.axis_size("rec"))
-    count = len(orders(*sizes)[0])
-    vmem = pl.BlockSpec(memory_space=pltpu.VMEM)
-    return pl.pallas_call(
-        lambda *refs: reduce_kernel(sizes, *refs),
-        out_shape=[jax.ShapeDtypeStruct(v.shape, v.dtype) for v in (g, x)],
-        in_specs=[vmem, vmem],
-        out_specs=[vmem, vmem],
-        scratch_shapes=[
-            pltpu.VMEM(g.shape, jnp.float32),
-            pltpu.VMEM(x.shape, jnp.float32),
-            pltpu.SemaphoreType.DMA((2, 2 * count)),
-            pltpu.SemaphoreType.DMA((2, 2 * count)),
-        ],
-        compiler_params=pltpu.CompilerParams(collective_id=0, has_side_effects=True),
-    )(g, x)
-
-
 def pairs(n):
     return [(i, j) for i in range(n) for j in range(i, n)]
 
@@ -207,7 +173,30 @@
     return jnp.broadcast_to(totals[i:i + 1], (TILE, TILE)).T
 
 
-def solve_kernel(frames, g_ref, x_ref, y_ref, a_ref, inv_ref, w_ref, c_ref):
+def timetable(x, spots):
+    total = x.plan[0][0][4]
+    costs = [1 + 8 * send[4] / total for send, _ in x.plan[1:]]
+    table, spent = {}, 0.0
+    for at, cost in enumerate(costs[:-1], 1):
+        spent += cost
+        spot = min(spots - 1, math.ceil(spent / sum(costs) * spots) - 1)
+        table.setdefault(spot, []).append(at)
+    return table
+
+
+def fused_kernel(sizes, frames, g_in, x_in, y_ref, g_ref, x_ref, g_box, x_box, a_ref, inv_ref, w_ref, c_ref, g_sem, x_sem):
+    one, two = orders(*sizes)
+    greet(one)
+    g = Stream(one, g_in, g_ref, g_box, g_sem)
+    x = Stream(two, x_in, x_ref, x_box, x_sem)
+    g.start(0)
+    for at in range(len(g.plan)):
+        g.finish(at)
+        g.start(at + 1)
+        if at == 0:
+            x.start(0)
+    x.finish(0)
+    x.start(1)
     size, n = a_ref.shape[0], a_ref.shape[0] // TILE
     m = y_ref.shape[1] // TILE
     units = TILE // 8
@@ -221,27 +210,51 @@
         if i == j:
             v = v + jnp.where(eye, RIDGE, 0.0)
         a_ref[i * TILE:(i + 1) * TILE, j * TILE:(j + 1) * TILE] = v
-    factor(a_ref, inv_ref, w_ref, TILE)
+    table = timetable(x, n * POINTS)
+
+    def hook(k, point):
+        for c in range(n):
+            stages = table.get(c * POINTS + point, [])
+            if stages:
+                @pl.when(k == c)
+                def _():
+                    for at in stages:
+                        x.finish(at)
+                        x.start(at + 1)
+
+    factor(a_ref, inv_ref, w_ref, TILE, hook)
+    x.finish(len(x.plan) - 1)
+    totals = g_ref[first:first + rows].reshape(8 * rows, TILE)
     for i in range(n):
+        col = column(totals, i)
         for j in range(m):
-            v = tile_at(x_ref, i * m + j) - cols[i] * totals[n + j:n + j + 1] / frames
+            v = tile_at(x_ref, i * m + j) - col * totals[n + j:n + j + 1] / frames
             c_ref[i * TILE:(i + 1) * TILE, j * TILE:(j + 1) * TILE] = v / math.sqrt(frames)
     substitute(a_ref, inv_ref, w_ref, c_ref, y_ref, TILE)
 
 
-def solve(g, x, size, wide, frames):
+def reduce_and_solve(g, x, size, wide, frames):
+    sizes = (lax.axis_size("frame"), lax.axis_size("rec"))
+    count = len(orders(*sizes)[0])
     vmem = pl.BlockSpec(memory_space=pltpu.VMEM)
     return pl.pallas_call(
-        lambda *refs: solve_kernel(frames, *refs),
+        lambda *refs: fused_kernel(sizes, frames, *refs),
         out_shape=jax.ShapeDtypeStruct((size, wide), jnp.float32),
         in_specs=[vmem, vmem],
         out_specs=vmem,
         scratch_shapes=[
+            pltpu.VMEM(g.shape, jnp.float32),
+            pltpu.VMEM(x.shape, jnp.float32),
+            pltpu.VMEM(g.shape, jnp.float32),
+            pltpu.VMEM(x.shape, jnp.float32),
             pltpu.VMEM((size, size), jnp.float32),
             pltpu.VMEM((size, TILE), jnp.float32),
             pltpu.VMEM((size, size), jnp.float32),
             pltpu.VMEM((size, wide), jnp.float32),
+            pltpu.SemaphoreType.DMA((2, 2 * count)),
+            pltpu.SemaphoreType.DMA((2, 2 * count)),
         ],
+        compiler_params=pltpu.CompilerParams(collective_id=0, has_side_effects=True),
     )(g, x)
 
 
@@ -301,8 +314,7 @@
     sums = jnp.pad(sums, ((0, -(n + m) % 8), (0, 0))).reshape(-1, 8, TILE)
     g = pad_units(jnp.concatenate([gram, sums]), devices)
     x = pad_units(blocks[:, n:].reshape(-1, 8, TILE), devices)
-    g, x = reduce_all(g, x)
-    return (features[None], solve(g, x, feat_width, wide, frames))
+    return (features[None], reduce_and_solve(g, x, feat_width, wide, frames))
 
 
 def solution(mesh):

time: 119 us -> 127 us (1.067)
  Pallas kernels: 87.3 us -> 92.8 us
  local copies, waits for them, and re-layouts: 11.9 us -> 14.2 us
    pallas_call x2 -> x1, Pallas kernels: 87.3 us -> 92.8 us  [reduce_and_solve(): pl.pallas_call(lambda *refs: fused_kernel(sizes, frames, *refs), out_shap...]
    unnamed x20 -> x21, local copies, waits for them, and re-layouts: 8.59 us -> 10.8 us
  transfers between devices with their start and end apart: 2 -> 2, of which waited for: 0 -> 0; matrix products, arithmetic and copies ran while one was open for 7% -> 6% of each run, Pallas kernels for 0% -> 0%
where the time goes in v1:
time: 127 us
  Pallas kernels  92.8 us (73%)
  local copies, waits for them, and re-layouts  14.2 us (11%)
  matrix products  8.84 us (7%)
  starting transfers between devices  6.15 us (5%)
  other arithmetic  4.02 us (3%)
    pallas_call x1, Pallas kernels, reduce_and_solve(): pl.pallas_call(lambda *refs: fused_kernel(sizes, frames, *refs), out_shap...  92.8 us
    unnamed x21, local copies, waits for them, and re-layouts  10.8 us
    dot_general x1, matrix products, per_device(): jnp.dot(stacked, flat_weight, preferred_element_type=jnp.float32)  7.55 us
    ppermute x1, starting transfers between devices, padded_2(): before = lax.ppermute(last, axis, up)  4.86 us
  transfers between devices with their start and end apart: 2, of which 0 were waited for; matrix products, arithmetic and copies ran while one was open for 6% of the time, Pallas kernels for 0%

profile of v1, /device:TPU:0, one launch (start us, length us, event | category | flops | bytes accessed | tf_op | source)
XLA Modules:
  0.0 126.9 jit_solution(4528888810157914814)
XLA Ops:
  0.6 0.0 copy-start
  0.6 0.9 fusion.26
  1.5 4.9 %collective-permute-start = (bf16[1,2,512]{2,1,0:T(2,128)(2,1)S(1)}, bf16[1,2,512]{2,1,0:T(2,128)(2,1)S(1)}, u32[]{:S(2)}, u32[]{:S(2)}) collective-permute-start(bf16[1,2,512]{2,1,0:T(2,128)(2,1)S(1)} %get-tuple-element.10), channel_id=1, source_target_pairs={{0,4},{4,8},{8,12},{12,16},{16,20},{20,24},{24,28},{1,5},{5,9},{9,... | collective-permute-start | bytes 6152 | tf_op jit(solution)/shard_map/ppermute | solution.py:273
  6.4 1.3 %collective-permute-start.1 = (bf16[1,2,512]{2,1,0:T(2,128)(2,1)S(1)}, bf16[1,2,512]{2,1,0:T(2,128)(2,1)S(1)}, u32[]{:S(2)}, u32[]{:S(2)}) collective-permute-start(bf16[1,2,512]{2,1,0:T(2,128)(2,1)S(1)} %get-tuple-element.9), channel_id=1, source_target_pairs={{4,0},{8,4},{12,8},{16,12},{20,16},{24,20},{28,24},{5,1},{9,5},{13... | collective-permute-start | bytes 6152 | tf_op jit(solution)/shard_map/ppermute | solution.py:274
  7.7 2.3 %constant_dynamic-update-slice_fusion.1 = bf16[1,1026,512]{2,1,0:T(8,128)(2,1)} fusion(bf16[1,1024,512]{2,1,0:T(8,128)(2,1)} %param.5), kind=kLoop, calls=%fused_computation.46 | loop fusion | bytes 2097152
  10.0 2.9 %copy.7 = s32[1,1024,512]{1,2,0:T(8,128)} copy(s32[1,1024,512]{2,1,0:T(8,128)} %param.8) | data formatting | bytes 4194304 | tf_op args[3]
  12.9 1.9 %convert_bitcast_fusion = bf16[1024,512]{0,1:T(8,128)(2,1)S(1)} fusion(s32[1,1024,512]{1,2,0:T(8,128)} %copy.7), kind=kLoop, calls=%fused_computation.42 | loop fusion | flops 524288 | bytes 3145728 | tf_op jit(solution)/shard_map/convert_element_type | solution.py:302
  14.8 0.0 copy-done.4
  14.9 0.1 compare_reduce_fusion
  14.9 0.0 collective-permute-done
  14.9 0.0 copy-done.1
  14.9 0.3 fusion.15
  15.3 0.0 copy-start.2
  15.3 0.3 fusion.22
  15.7 0.3 fusion.23
  16.0 0.0 collective-permute-done.1
  16.0 0.5 copy-done.2
  16.5 0.3 fusion.19
  16.9 0.3 fusion.17
  17.2 0.0 copy-done
  17.2 0.0 copy-done.5
  17.3 7.5 %fusion.2 = bf16[1024,512]{0,1:T(8,128)(2,1)S(1)} fusion(bf16[1024,2560]{1,0:T(8,128)(2,1)S(1)} %fusion.17, bf16[2560,512]{1,0:T(8,128)(2,1)S(1)} %bitcast.52, f32[512]{0:T(512)S(1)} %copy-done.5), kind=kOutput, calls=%fused_computation.4 | convolution fusion | flops 2718957568 | bytes 8914944 | tf_op jit(solution)/shard_map/dot_general | solution.py:300
  24.8 0.0 copy-start.3
  24.8 1.3 %fusion.11 = f32[64,8,8,128]{3,1,2,0:T(8,128)S(1)} fusion(bf16[1024,512]{0,1:T(8,128)(2,1)S(1)} %fusion.2, bf16[1024,512]{0,1:T(8,128)(2,1)S(1)} %convert_bitcast_fusion), kind=kOutput, calls=%fused_computation.23 | convolution fusion | flops 1077936128 | bytes 4194304 | tf_op jit(solution)/shard_map/dot_general | solution.py:303
  26.1 0.5 copy.10
  26.6 0.4 copy.12
  27.1 0.3 convert_reduce_fusion
  27.4 1.0 slice.64
  28.5 1.0 pad.4.refs_0_
  29.5 92.8 %shard_map.68 = f32[512,512]{1,0:T(8,128)} custom-call(f32[192,8,128]{2,1,0:T(8,128)} %pad.4.refs_0_, f32[256,8,128]{2,1,0:T(8,128)} %bitcast.60), custom_call_target="tpu_custom_call" | custom-call | tf_op jit(solution)/shard_map/pallas_call | solution.py:240
  122.3 2.3 %copy.9 = bf16[1,1024,512]{2,1,0:T(8,128)(2,1)} copy(bf16[1,1024,512]{1,2,0:T(8,128)(2,1)} %bitcast.59) | data formatting | bytes 2097152
  124.6 2.3 %copy.23 = f32[512,512]{1,0:T(8,128)} copy(f32[512,512]{1,0:T(8,128)} %shard_map.68) | data formatting | bytes 2097152
  (13 shorter events, 0.1 us)
Async XLA Ops:
  0.6 16.6 %copy-start = (bf16[5,512,512]{2,1,0:T(8,128)(2,1)S(1)}, bf16[5,512,512]{2,1,0:T(8,128)(2,1)}, u32[]{:S(2)}) copy-start(bf16[5,512,512]{2,1,0:T(8,128)(2,1)} %param.6) | copy-start | bytes 7864324
  1.5 13.4 %collective-permute-start = (bf16[1,2,512]{2,1,0:T(2,128)(2,1)S(1)}, bf16[1,2,512]{2,1,0:T(2,128)(2,1)S(1)}, u32[]{:S(2)}, u32[]{:S(2)}) collective-permute-start(bf16[1,2,512]{2,1,0:T(2,128)(2,1)S(1)} %get-tuple-element.10), channel_id=1, source_target_pairs={{0,4},{4,8},{8,12},{12,16},{16,20},{20,24},{24,28},{1,5},{5,9},{9,... | collective-permute-start | bytes 6152 | tf_op jit(solution)/shard_map/ppermute | solution.py:273
  6.4 9.6 %collective-permute-start.1 = (bf16[1,2,512]{2,1,0:T(2,128)(2,1)S(1)}, bf16[1,2,512]{2,1,0:T(2,128)(2,1)S(1)}, u32[]{:S(2)}, u32[]{:S(2)}) collective-permute-start(bf16[1,2,512]{2,1,0:T(2,128)(2,1)S(1)} %get-tuple-element.9), channel_id=1, source_target_pairs={{4,0},{8,4},{12,8},{16,12},{20,16},{24,20},{28,24},{5,1},{9,5},{13... | collective-permute-start | bytes 6152 | tf_op jit(solution)/shard_map/ppermute | solution.py:274
  12.9 1.9 %copy-start.4 = (s32[2,1,1024]{2,1,0:T(1,128)S(1)}, s32[2,1,1024]{2,1,0:T(1,128)}, u32[]{:S(2)}) copy-start(s32[2,1,1024]{2,1,0:T(1,128)} %param.9) | copy-start | bytes 24580
  12.9 2.0 %copy-start.1 = (bf16[1,1024,512]{2,1,0:T(8,128)(2,1)S(1)}, bf16[1,1024,512]{2,1,0:T(8,128)(2,1)}, u32[]{:S(2)}) copy-start(bf16[1,1024,512]{2,1,0:T(8,128)(2,1)} %param.5) | copy-start | bytes 3145732
  15.3 1.2 copy-start.2
  16.5 0.7 copy-start.5
  24.8 2.2 %copy-start.3 = (bf16[1024,512]{0,1:T(8,128)(2,1)}, bf16[1024,512]{0,1:T(8,128)(2,1)S(1)}, u32[]{:S(2)}) copy-start(bf16[1024,512]{0,1:T(8,128)(2,1)S(1)} %fusion.2) | copy-start | bytes 3145732
